TPU v7x, 32 devices: a whole 2x2x4 slice. The times are simulated.
32 devices in a mesh: clip: 2 (over y), patch: 4 (over z), head: 2 (over x), rep: 2 (over core).
Axes of the slice: x: 2, y: 2, z: 4, core: 2. Of those that a mesh axis runs over, the one named last changes fastest.
Arguments:
- tokens: bfloat16 [1024, 3072], P(('clip', 'patch', 'head', 'rep')), parts along dimension 0, may hold values from -24 to 24
- modulation: float32 [3, 3072], replicated, may hold values from -3 to 3
- in_weight: bfloat16 [3072, 16, 384], P(None, ('head', 'rep')), may hold values from -0.109375 to 0.109375
- query_gain: float32 [128], replicated, may hold values from 1 to 2.5
- key_gain: float32 [128], replicated, may hold values from 0.25 to 1.75
- out_weight: bfloat16 [16, 128, 3072], P(('head', 'rep')), may hold values from -1.5 to 1.5
- stale_cache: bfloat16 [1024, 16, 256], P(('clip', 'patch', 'head', 'rep')), parts along dimension 0, may hold values from -440 to 440, as said below
- lengths: int32 [8], P('clip'), parts along dimension 0, may hold values from 1 to 128, 384 in all
Outputs:
- update: bfloat16 [1024, 3072], P(('clip', 'patch', 'head', 'rep')), parts along dimension 0
- new_cache: bfloat16 [1024, 16, 256], P(('clip', 'patch', 'head', 'rep')), parts along dimension 0
There are 2 independent parts, one for each index of `clip`. A program takes and returns all parts, laid end to end along the dimension named above; an argument that names none is the same for every part. Nothing has to cross between parts.
Inputs may be any that keep to these rules, and one draw needn't show every extreme that they name: stale_cache[s, h] holds the stale key of token s and head h in its first 128 entries and the stale value in its last 128. Only the first lengths[p] tokens of patch p are live keys.
All inputs are finite; a program needn't handle non-finite values.
Results may differ from a plain program's by a relative error of at most 0.02.
The roundings to bfloat16 on the way count: a program that leaves them out, or rounds other values in their place, can miss the bound.
Values may be sent and summed in bfloat16 or wider, within the bound.
No kernel may reach another device: no remote copies, remote signals or barrier semaphores. Data moves between devices by JAX's collectives and lax.ppermute only.
A program may use at most 128 MiB of HBM per device.

v0:
```python
import math
import jax
import jax.numpy as jnp
from jax import lax
from jax.sharding import PartitionSpec as P

EPSILON = 1e-06
NEGATIVE = -1e30
key_block = 512


def normalize_rows(values):
    average = jnp.mean(values, axis=-1, keepdims=True)
    centred = values - average
    variance = jnp.mean(centred * centred, axis=-1, keepdims=True)
    return centred * lax.rsqrt(variance + EPSILON)


def rms_gain(values, gain):
    return values * lax.rsqrt(jnp.mean(values * values, axis=-1, keepdims=True) + EPSILON) * gain


def project(normed, in_weight, query_gain, key_gain):
    row_count = normed.shape[0]
    head_count = in_weight.shape[1]
    triple = in_weight.shape[2]
    head_dim = triple // 3
    flat_weight = in_weight.reshape(in_weight.shape[0], head_count * triple)
    projected = jnp.dot(normed, flat_weight, preferred_element_type=jnp.float32).reshape(
        row_count, head_count, triple
    )
    queries = rms_gain(projected[..., :head_dim], query_gain)
    fresh_keys = rms_gain(projected[..., head_dim : 2 * head_dim], key_gain)
    return jnp.concatenate([queries, fresh_keys, projected[..., 2 * head_dim :]], axis=-1).astype(
        jnp.bfloat16
    )


def lookup(lengths, patch_of):
    patch_ids = jnp.arange(lengths.shape[0], dtype=jnp.int32)
    return jnp.sum(jnp.where(patch_of[:, None] == patch_ids[None, :], lengths[None, :], 0), axis=1)


def attend(running, queries, key_rows, usable):
    head_dim = queries.shape[-1]
    row_max, denominator, weighted = running
    scores = jnp.einsum(
        "qhd,khd->qhk", queries, key_rows[..., :head_dim], preferred_element_type=jnp.float32
    )
    scores = scores * (1.0 / math.sqrt(head_dim))
    key_mask = usable[None, None, :]
    scores = jnp.where(key_mask, scores, NEGATIVE)
    new_max = jnp.maximum(row_max, jnp.max(scores, axis=-1))
    weights = jnp.where(key_mask, jnp.exp(scores - new_max[..., None]), 0.0)
    factor = jnp.exp(row_max - new_max)
    denominator = denominator * factor + jnp.sum(weights, axis=-1)
    weighted = weighted * factor[..., None] + jnp.einsum(
        "qhk,khd->qhd",
        weights.astype(jnp.bfloat16),
        key_rows[..., head_dim:],
        preferred_element_type=jnp.float32,
    )
    return (new_max, denominator, weighted)


def attend_blocks(running, queries, key_rows, usable):
    key_count = key_rows.shape[0]
    if key_count > key_block and key_count % key_block == 0:
        shaped = key_rows.reshape((key_count // key_block, key_block) + key_rows.shape[1:])
        usable_rows = usable.reshape(key_count // key_block, key_block)

        def step_block(current, operands):
            return (attend(current, queries, operands[0], operands[1]), None)

        running, _ = lax.scan(step_block, running, (shaped, usable_rows))
        return running
    return attend(running, queries, key_rows, usable)


def per_device(
    tokens, modulation, in_weight, query_gain, key_gain, out_weight, stale_cache, lengths
):
    heads_dev = in_weight.shape[1]
    head_dim = query_gain.shape[0]
    normed = (
        normalize_rows(tokens.astype(jnp.float32)) * (1.0 + modulation[1]) + modulation[0]
    ).astype(jnp.bfloat16)
    fresh = project(
        lax.all_gather(normed, ("head", "rep"), axis=0, tiled=True), in_weight, query_gain, key_gain
    )
    queries = fresh[..., :head_dim]
    own_rows = fresh[..., head_dim:]
    new_cache = lax.all_to_all(own_rows, ("head", "rep"), split_axis=0, concat_axis=1, tiled=True)
    patch_tok = fresh.shape[0]
    own_patch = lax.axis_index("patch")
    own_length = lookup(lengths, jnp.full((1,), own_patch, jnp.int32))[0]
    running = (
        jnp.full((patch_tok, heads_dev), NEGATIVE, jnp.float32),
        jnp.zeros((patch_tok, heads_dev), jnp.float32),
        jnp.zeros((patch_tok, heads_dev, head_dim), jnp.float32),
    )
    running = attend_blocks(
        running, queries, own_rows, jnp.arange(patch_tok, dtype=jnp.int32) < own_length
    )
    stale_heads = lax.all_to_all(
        stale_cache, ("head", "rep"), split_axis=1, concat_axis=0, tiled=True
    )
    shard_part = lax.all_gather(stale_heads, "patch", axis=0, tiled=True)
    key_index = jnp.arange(shard_part.shape[0], dtype=jnp.int32)
    patch_of = key_index // patch_tok
    position = key_index % patch_tok
    usable = (position < lookup(lengths, patch_of)) & (patch_of != own_patch)
    running = attend_blocks(running, queries, shard_part, usable)
    attended = (running[2] / running[1][..., None]).astype(jnp.bfloat16)
    flat_rows = attended.reshape(patch_tok, heads_dev * head_dim)
    flat_weight = out_weight.reshape(heads_dev * head_dim, out_weight.shape[2])
    attention = lax.psum_scatter(
        jnp.dot(flat_rows, flat_weight, preferred_element_type=jnp.float32).astype(jnp.bfloat16),
        ("head", "rep"),
        scatter_dimension=0,
        tiled=True,
    ).astype(jnp.float32)
    update = (modulation[2] * attention).astype(jnp.bfloat16)
    return (update, new_cache)


def solution(mesh):
    return jax.shard_map(
        per_device,
        mesh=mesh,
        in_specs=(
            P(("clip", "patch", "head", "rep"), None),
            P(),
            P(None, ("head", "rep"), None),
            P(),
            P(),
            P(("head", "rep"), None, None),
            P(("clip", "patch", "head", "rep"), None, None),
            P("clip"),
        ),
        out_specs=(
            P(("clip", "patch", "head", "rep"), None),
            P(("clip", "patch", "head", "rep"), None, None),
        ),
        check_vma=False,
    )
```

profile of v0, /device:TPU:0, one launch (start us, length us, event | category | flops | bytes accessed | tf_op | source)
XLA Modules:
  0.0 127.5 jit_solution(7977245236789460566)
XLA Ops:
  7.2 1.9 %copy.21 = bf16[32,16,256]{2,0,1:T(8,128)(2,1)} copy(bf16[32,16,256]{2,1,0:T(8,128)(2,1)} %param.14) | data formatting | bytes 524288 | tf_op args[6]
  9.1 4.2 %all-to-all-start = ((bf16[32,16,256]{2,0,1:T(8,128)(2,1)}), bf16[32,16,256]{2,0,1:T(8,128)(2,1)}, u32[]{:S(2)}, u32[]{:S(2)}) async-start(bf16[32,16,256]{2,0,1:T(8,128)(2,1)} %copy.21), calls=%async_computation | async-start | bytes 524288 | tf_op jit(solution)/shard_map/all_to_all | solution.py:105
  13.3 9.0 %copy.31 = bf16[384,8,4,384]{3,1,2,0:T(8,128)(2,1)} copy(bf16[384,8,4,384]{3,2,1,0:T(4,128)(2,1)} %bitcast.47) | data formatting | bytes 18874368
  22.3 12.7 %copy.18 = bf16[1536,3072]{1,0:T(8,128)(2,1)} copy(bf16[1536,3072]{0,1:T(8,128)(2,1)} %bitcast.46) | data formatting | bytes 18874368 | tf_op jit(solution)/shard_map/dot_general | solution.py:29
  35.6 9.9 %all_gather.6 = bf16[128,3072]{1,0:T(8,128)(2,1)S(1)} all-gather(bf16[32,3072]{1,0:T(8,128)(2,1)S(1)} %fusion.30), channel_id=1, replica_groups=mesh['clip'=2,'patch'=4,'head'=2,'rep'=2] {'head','rep'}, dimensions={0}, use_global_device_ids=true | all-gather | bytes 983040 | tf_op jit(solution)/shard_map/all_gather | solution.py:89
  45.6 7.8 %fusion.12 = f32[128,4,384]{2,0,1:T(8,128)} fusion(bf16[4,384,3072]{2,1,0:T(8,128)(2,1)} %bitcast.45, bf16[128,3072]{1,0:T(8,128)(2,1)S(1)} %all_gather.6), kind=kOutput, calls=%fused_computation.18 | convolution fusion | flops 1207959552 | bytes 11010048 | tf_op jit(solution)/shard_map/dot_general | solution.py:29
  54.0 1.7 %copy.22 = bf16[32,4,4,256]{3,0,1,2:T(8,128)(2,1)} copy(bf16[32,4,4,256]{3,0,2,1:T(8,128)(2,1)} %bitcast.8) | data formatting | bytes 524288 | tf_op jit(solution)/shard_map/all_to_all | solution.py:105
  55.7 0.7 iota_compare_fusion.1
  56.5 1.2 multiply_reduce_fusion
  58.4 1.1 multiply_convert_fusion.2
  59.5 1.8 %fusion.50 = (f32[128,4]{0,1:T(4,128)}, f32[128,4,128]{0,2,1:T(8,128)S(1)}) fusion(bf16[128,4,128]{2,0,1:T(8,128)(2,1)S(1)} %multiply_convert_fusion.2, f32[128,4,384]{2,0,1:T(8,128)} %fusion.12, f32[128]{0:T(128)} %param.11, f32[128,4]{0,1:T(4,128)S(1)} %add_rsqrt_fusion, pred[128]{0:T(512)(128)(4,1)S(1)} %iota_compare_fusion.1), kind=kOutput, calls=%fused_computation.77 | convolution fusion | flops 17169920 | bytes 660096 | tf_op jit(solution)/shard_map/qhd,khd->qhk/dot_general | solution.py:47
  61.3 24.1 %all-gather.2.cloned.1.call-done = bf16[512,4,256]{2,0,1:T(8,128)(2,1)} async-done(((bf16[128,4,256]{2,0,1:T(8,128)(2,1)}), bf16[512,4,256]{2,0,1:T(8,128)(2,1)}) %all-gather.2.cloned.1.call-update) | async-done | bytes 1048592 | tf_op jit(solution)/shard_map/all_gather | solution.py:108
  85.4 1.6 %fusion.51 = (f32[128,4]{0,1:T(4,128)S(1)}, f32[128,4,512]{2,0,1:T(8,128)S(1)}) fusion(bf16[512,4,256]{2,0,1:T(8,128)(2,1)} %all-gather.2.cloned.1.call-done, f32[128,4,384]{2,0,1:T(8,128)} %fusion.12, f32[128]{0:T(128)} %param.11, f32[128,4]{0,1:T(4,128)S(1)} %add_rsqrt_fusion, pred[512]{0:T(512)(128)(4,1)} %compare_and_fusion), kind=kOutput, calls=%fused_computation.78 | convolution fusion | flops 68091392 | bytes 1840128 | tf_op jit(solution)/shard_map/qhd,khd->qhk/dot_general | solution.py:47
  87.0 0.7 exponential_multiply_fusion
  88.0 1.0 fusion.10
  89.0 0.7 fusion.31
  89.7 1.3 %multiply_add_fusion = (f32[128,4]{0,1:T(4,128)}, f32[128,4]{0,1:T(4,128)S(1)}) fusion(f32[128,4]{0,1:T(4,128)S(1)} %fusion.10, f32[128,4]{0,1:T(4,128)S(1)} %fusion.31, f32[128,4]{0,1:T(4,128)} %get-tuple-element.12, f32[128,4]{0,1:T(4,128)S(1)} %get-tuple-element.14), kind=kLoop, calls=%fused_computation.56 | loop fusion | flops 4096 | bytes 12288 | tf_op jit(solution)/shard_map/add | solution.py:56
  91.0 1.9 %fusion.7 = f32[128,4,128]{0,2,1:T(8,128)} fusion(f32[128,4,128]{0,2,1:T(8,128)S(1)} %get-tuple-element.13, f32[128,4]{0,1:T(4,128)S(1)} %get-tuple-element.5, f32[128,4]{0,1:T(4,128)S(1)} %get-tuple-element.11, f32[128,4]{0,1:T(4,128)S(1)} %get-tuple-element.9, pred[128]{0:T(512)(128)(4,1)} %copy-done.4, f32[128,4,384]{2,0,1:T(8,128)} %fusion.12), kind=kOutput, calls=%fused_computation.12 | convolution fusion | flops 17104896 | bytes 662016 | tf_op jit(solution)/shard_map/qhk,khd->qhd/dot_general | solution.py:57
  92.9 3.3 %fusion = bf16[128,3072]{1,0:T(8,128)(2,1)} fusion(bf16[4,128,3072]{2,1,0:T(8,128)(2,1)S(1)} %copy-done, f32[128,4,128]{0,2,1:T(8,128)} %fusion.7, f32[128,4,512]{2,0,1:T(8,128)} %copy-done.1, bf16[512,4,256]{2,0,1:T(8,128)(2,1)} %all-gather.2.cloned.1.call-done, f32[128,4]{0,1:T(4,128)S(1)} %get-tuple-element.10, pred[512]{0:T(512)(128)(4,1)} %compare_and_fusion, ...), kind=kOutput, calls=%fused_computation.1 | convolution fusion | flops 471138304 | bytes 5771776 | tf_op jit(solution)/shard_map/dot_general | solution.py:118
  96.2 1.0 slice.68
  97.5 8.5 %all_to_all.36 = bf16[128,4,256]{2,1,0:T(4,128)(2,1)S(1)} all-to-all(bf16[128,4,256]{2,1,0:T(4,128)(2,1)S(1)} %copy.25), channel_id=1, replica_groups=mesh['clip'=2,'patch'=4,'head'=2,'rep'=2] {'head','rep'}, dimensions={0} | all-to-all | bytes 524288 | tf_op jit(solution)/shard_map/all_to_all | solution.py:93
  106.1 0.8 all_to_all.33
  106.9 12.1 %reduce-scatter.2.cloned.1.call-done = bf16[32,3072]{1,0:T(8,128)(2,1)} async-done(((bf16[128,3072]{1,0:T(8,128)(2,1)}), bf16[32,3072]{1,0:T(8,128)(2,1)}) %reduce-scatter.2.cloned.1.call-update) | async-done | bytes 196624 | tf_op jit(solution)/shard_map/reduce_scatter | solution.py:117
  119.0 1.6 %multiply_convert_fusion = bf16[32,3072]{1,0:T(8,128)(2,1)} fusion(bf16[32,3072]{1,0:T(8,128)(2,1)} %reduce-scatter.2.cloned.1.call-done, f32[3072]{0:T(1024)S(1)} %bitcast.50), kind=kLoop, calls=%fused_computation.33 | loop fusion | flops 294912 | bytes 405504 | tf_op jit(solution)/shard_map/convert_element_type | solution.py:123
  (34 shorter events, 2.6 us)
Async XLA Ops:
  7.2 85.8 %copy-start = (bf16[4,128,3072]{2,1,0:T(8,128)(2,1)S(1)}, bf16[4,128,3072]{2,1,0:T(8,128)(2,1)}, u32[]{:S(2)}) copy-start(bf16[4,128,3072]{2,1,0:T(8,128)(2,1)} %param.13) | copy-start | bytes 9437188
  9.1 44.9 %all-to-all-start = ((bf16[32,16,256]{2,0,1:T(8,128)(2,1)}), bf16[32,16,256]{2,0,1:T(8,128)(2,1)}, u32[]{:S(2)}, u32[]{:S(2)}) async-start(bf16[32,16,256]{2,0,1:T(8,128)(2,1)} %copy.21), calls=%async_computation | async-start | bytes 524288 | tf_op jit(solution)/shard_map/all_to_all | solution.py:105
  13.3 72.1 %all-gather.2.cloned.1.call-start = ((), (), s32[]{:S(2)}) async-start(), calls=%async_computation.3 | async-start | bytes 1310720 | tf_op jit(solution)/shard_map/all_gather | solution.py:108
  22.3 12.7 %copy-start.3 = (f32[3,3072]{1,0:T(4,128)S(1)}, f32[3,3072]{1,0:T(4,128)}, u32[]{:S(2)}) copy-start(f32[3,3072]{1,0:T(4,128)} %param.9) | copy-start | bytes 110596
  22.3 12.8 %copy-start.2 = (bf16[32,3072]{1,0:T(8,128)(2,1)S(1)}, bf16[32,3072]{1,0:T(8,128)(2,1)}, u32[]{:S(2)}) copy-start(bf16[32,3072]{1,0:T(8,128)(2,1)} %param.8) | copy-start | bytes 589828
  35.0 18.3 %copy-start.6 = (s32[4]{0:T(128)S(1)}, s32[4]{0:T(128)}, u32[]{:S(2)}) copy-start(s32[4]{0:T(128)} %param.15) | copy-start | bytes 52
  35.1 23.3 %copy-start.5 = (f32[128]{0:T(128)S(1)}, f32[128]{0:T(128)}, u32[]{:S(2)}) copy-start(f32[128]{0:T(128)} %param.12) | copy-start | bytes 1540
  55.7 63.3 %reduce-scatter.2.cloned.1.call-start = ((), (), s32[]{:S(2)}) async-start(), calls=%async_computation.4 | async-start | bytes 983040 | tf_op jit(solution)/shard_map/reduce_scatter | solution.py:117
  56.4 3.1 %copy-start.4 = (pred[128]{0:T(512)(128)(4,1)}, pred[128]{0:T(512)(128)(4,1)S(1)}, u32[]{:S(2)}) copy-start(pred[128]{0:T(512)(128)(4,1)S(1)} %iota_compare_fusion.1) | copy-start | bytes 388
  87.0 1.0 copy-start.1
Sparse Core Ops, SparseCore 0:
  55.8 29.5 all-gather.1
  96.4 22.5 reduce-scatter.1
where the time goes:
time: 128 us; the launch traced here: 127 us
  waiting for transfers between devices  36.3 us (28%)
  local copies, waits for them, and re-layouts  27.7 us (22%)
  blocking collectives  18.5 us (14%)
  matrix products  16.4 us (13%)
  between operations  14.2 us (11%)
  other arithmetic  10.2 us (8%)
  starting transfers between devices  4.28 us (3%)
    all_gather x1, waiting for transfers between devices, per_device(): shard_part = lax.all_gather(stale_heads, 'patch', axis=0, tiled=True)  24.1 us
    dot_general x1, local copies, waits for them, and re-layouts, project(): jnp.dot(normed, flat_weight, preferred_element_type=jnp.float32)  12.7 us
    reduce_scatter x1, waiting for transfers between devices, per_device(): lax.psum_scatter(jnp.dot(flat_rows, flat_weight, preferred_element_type=j...  12.1 us
    unnamed x16, local copies, waits for them, and re-layouts  11.2 us
    all_gather x1, blocking collectives, per_device(): lax.all_gather(normed, ('head', 'rep'), axis=0, tiled=True)  9.92 us
    all_to_all x1, blocking collectives, per_device(): lax.all_to_all(own_rows, ('head', 'rep'), split_axis=0, concat_axis=1, ti...  8.54 us
    dot_general x1, matrix products, project(): jnp.dot(normed, flat_weight, preferred_element_type=jnp.float32)  7.79 us
    all_to_all x1, starting transfers between devices, per_device(): lax.all_to_all(stale_cache, ('head', 'rep'), split_axis=1, concat_axis=0,...  4.24 us
  transfers between devices with their start and end apart: 3, of which 2 were waited for; matrix products, arithmetic and copies ran while one was open for 29% of the time, Pallas kernels for 0%

commit v1 on v0

--- a/solution.py
+++ b/solution.py
@@ -105,7 +105,14 @@
     stale_heads = lax.all_to_all(
         stale_cache, ("head", "rep"), split_axis=1, concat_axis=0, tiled=True
     )
-    shard_part = lax.all_gather(stale_heads, "patch", axis=0, tiled=True)
+    ring = [stale_heads]
+    for hop in range(3):
+        ring.append(lax.ppermute(ring[-1], "patch", [(dev, (dev + 1) % 4) for dev in range(4)]))
+    shard_part = jnp.roll(
+        jnp.concatenate(ring[::-1], axis=0),
+        (lax.axis_index("patch") + 1) * ring[0].shape[0],
+        axis=0,
+    )
     key_index = jnp.arange(shard_part.shape[0], dtype=jnp.int32)
     patch_of = key_index // patch_tok
     position = key_index % patch_tok

time: 128 us -> 127 us (level)
  local copies, waits for them, and re-layouts: 27.7 us -> 34.3 us
  matrix products: 16.4 us -> 12.2 us
  waiting for transfers between devices: 36.3 us -> 33 us
  other arithmetic: 10.2 us -> 7.44 us
  starting transfers between devices: 4.28 us -> 6.31 us
    all_gather x1 -> x0, waiting for transfers between devices: 24.1 us -> none  [per_device(): shard_part = lax.all_gather(stale_heads, 'patch', axis=0, tiled=True)]
    ppermute x0 -> x3, waiting for transfers between devices: none -> 22.5 us  [per_device(): lax.ppermute(ring[-1], 'patch', [(dev, (dev + 1) % 4) for dev in range(4)])]
    unnamed x16 -> x35, local copies, waits for them, and re-layouts: 11.2 us -> 18.6 us
    ppermute x0 -> x3, starting transfers between devices: none -> 2.07 us  [per_device(): lax.ppermute(ring[-1], 'patch', [(dev, (dev + 1) % 4) for dev in range(4)])]
    dot_general x2, matrix products: 3.42 us -> 1.71 us  [attend(): jnp.einsum('qhd,khd->qhk', queries, key_rows[..., :head_dim], preferred_e...]
    dot_general x1, matrix products: 1.92 us -> 0.27 us  [attend(): jnp.einsum('qhk,khd->qhd', weights.astype(jnp.bfloat16), key_rows[..., he...]
    reduce_scatter x1, waiting for transfers between devices: 12.1 us -> 10.5 us  [per_device(): lax.psum_scatter(jnp.dot(flat_rows, flat_weight, preferred_element_type=j...]
    reduce_sum x2, other arithmetic: 1.69 us -> 0.32 us  [attend(): denominator = denominator * factor + jnp.sum(weights, axis=-1)]
  transfers between devices with their start and end apart: 3 -> 5, of which waited for: 2 -> 4; matrix products, arithmetic and copies ran while one was open for 29% -> 29% of each run, Pallas kernels for 0% -> 0%
where the time goes in v1:
time: 127 us; the launch traced here: 126 us
  local copies, waits for them, and re-layouts  34.3 us (27%)
  waiting for transfers between devices  33 us (26%)
  blocking collectives  18.4 us (14%)
  between operations  14.3 us (11%)
  matrix products  12.2 us (10%)
  other arithmetic  7.44 us (6%)
  starting transfers between devices  6.31 us (5%)
    ppermute x3, waiting for transfers between devices, per_device(): lax.ppermute(ring[-1], 'patch', [(dev, (dev + 1) % 4) for dev in range(4)])  22.5 us
    unnamed x35, local copies, waits for them, and re-layouts  18.6 us
    dot_general x1, local copies, waits for them, and re-layouts, project(): jnp.dot(normed, flat_weight, preferred_element_type=jnp.float32)  12.7 us
    reduce_scatter x1, waiting for transfers between devices, per_device(): lax.psum_scatter(jnp.dot(flat_rows, flat_weight, preferred_element_type=j...  10.5 us
    all_gather x1, blocking collectives, per_device(): lax.all_gather(normed, ('head', 'rep'), axis=0, tiled=True)  9.93 us
    all_to_all x1, blocking collectives, per_device(): lax.all_to_all(own_rows, ('head', 'rep'), split_axis=0, concat_axis=1, ti...  8.43 us
    dot_general x1, matrix products, project(): jnp.dot(normed, flat_weight, preferred_element_type=jnp.float32)  6.91 us
    all_to_all x1, starting transfers between devices, per_device(): lax.all_to_all(stale_cache, ('head', 'rep'), split_axis=1, concat_axis=0,...  4.24 us
  transfers between devices with their start and end apart: 5, of which 4 were waited for; matrix products, arithmetic and copies ran while one was open for 29% of the time, Pallas kernels for 0%

profile of v1, /device:TPU:0, one launch (start us, length us, event | category | flops | bytes accessed | tf_op | source)
XLA Modules:
  0.0 125.9 jit_solution(1365148170852190958)
XLA Ops:
  7.2 1.9 %copy.21 = bf16[32,16,256]{2,0,1:T(8,128)(2,1)} copy(bf16[32,16,256]{2,1,0:T(8,128)(2,1)} %param.14) | data formatting | bytes 524288 | tf_op args[6]
  9.1 4.2 %all-to-all-start = ((bf16[32,16,256]{2,0,1:T(8,128)(2,1)}), bf16[32,16,256]{2,0,1:T(8,128)(2,1)}, u32[]{:S(2)}, u32[]{:S(2)}) async-start(bf16[32,16,256]{2,0,1:T(8,128)(2,1)} %copy.21), calls=%async_computation | async-start | bytes 524288 | tf_op jit(solution)/shard_map/all_to_all | solution.py:105
  13.3 9.0 %copy.33 = bf16[384,8,4,384]{3,1,2,0:T(8,128)(2,1)} copy(bf16[384,8,4,384]{3,2,1,0:T(4,128)(2,1)} %bitcast.47) | data formatting | bytes 18874368
  22.3 12.7 %copy.18 = bf16[1536,3072]{1,0:T(8,128)(2,1)} copy(bf16[1536,3072]{0,1:T(8,128)(2,1)} %bitcast.46) | data formatting | bytes 18874368 | tf_op jit(solution)/shard_map/dot_general | solution.py:29
  35.6 9.9 %all_gather.3 = bf16[128,3072]{1,0:T(8,128)(2,1)S(1)} all-gather(bf16[32,3072]{1,0:T(8,128)(2,1)S(1)} %fusion.30), channel_id=1, replica_groups=mesh['clip'=2,'patch'=4,'head'=2,'rep'=2] {'head','rep'}, dimensions={0}, use_global_device_ids=true | all-gather | bytes 983040 | tf_op jit(solution)/shard_map/all_gather | solution.py:89
  45.5 6.9 %fusion.12 = f32[128,4,384]{2,0,1:T(8,128)S(1)} fusion(bf16[4,384,3072]{2,1,0:T(8,128)(2,1)} %bitcast.45, bf16[128,3072]{1,0:T(8,128)(2,1)S(1)} %all_gather.3), kind=kOutput, calls=%fused_computation.18 | convolution fusion | flops 1207959552 | bytes 11010048 | tf_op jit(solution)/shard_map/dot_general | solution.py:29
  54.3 1.0 copy.22
  55.2 2.1 %collective-permute-start = (bf16[128,4,256]{2,0,1:T(8,128)(2,1)S(1)}, bf16[128,4,256]{2,0,1:T(8,128)(2,1)S(1)}, u32[]{:S(2)}, u32[]{:S(2)}) collective-permute-start(bf16[128,4,256]{2,0,1:T(8,128)(2,1)S(1)} %bitcast.48), channel_id=1, source_target_pairs={{0,4},{4,8},{8,12},{12,0},{1,5},{5,9},{9,13},{13,1},{2,6},{6,10},{... | collective-permute-start | bytes 786440 | tf_op jit(solution)/shard_map/ppermute | solution.py:110
  57.8 8.4 %collective-permute-done = bf16[128,4,256]{2,0,1:T(8,128)(2,1)S(1)} collective-permute-done((bf16[128,4,256]{2,0,1:T(8,128)(2,1)S(1)}, bf16[128,4,256]{2,0,1:T(8,128)(2,1)S(1)}, u32[]{:S(2)}, u32[]{:S(2)}) %collective-permute-start) | collective-permute-done | bytes 262176 | tf_op jit(solution)/shard_map/ppermute | solution.py:110
  67.5 1.1 multiply_convert_fusion.2
  68.6 7.4 %collective-permute-done.1 = bf16[128,4,256]{2,0,1:T(8,128)(2,1)} collective-permute-done((bf16[128,4,256]{2,0,1:T(8,128)(2,1)S(1)}, bf16[128,4,256]{2,0,1:T(8,128)(2,1)}, u32[]{:S(2)}, u32[]{:S(2)}) %collective-permute-start.1) | collective-permute-done | bytes 262176 | tf_op jit(solution)/shard_map/ppermute | solution.py:110
  76.0 1.1 iota_compare_fusion.1
  77.2 1.3 %fusion.53 = (f32[128,4]{0,1:T(4,128)S(1)}, f32[128,4,128]{0,2,1:T(8,128)S(1)}) fusion(bf16[128,4,128]{2,0,1:T(8,128)(2,1)S(1)} %multiply_convert_fusion.2, f32[128,4,384]{2,0,1:T(8,128)} %copy-done.2, f32[128]{0:T(128)} %param.11, f32[128,4]{0,1:T(4,128)S(1)} %add_rsqrt_fusion, pred[128]{0:T(512)(128)(4,1)} %iota_compare_fusion.1), kind=kOutput, calls=%fused_computation.87 | convolution fusion | flops 17169920 | bytes 660480 | tf_op jit(solution)/shard_map/qhd,khd->qhk/dot_general | solution.py:47
  78.5 6.8 %collective-permute-done.2 = bf16[128,4,256]{2,0,1:T(8,128)(2,1)} collective-permute-done((bf16[128,4,256]{2,0,1:T(8,128)(2,1)}, bf16[128,4,256]{2,0,1:T(8,128)(2,1)}, u32[]{:S(2)}, u32[]{:S(2)}) %collective-permute-start.2) | collective-permute-done | bytes 262176 | tf_op jit(solution)/shard_map/ppermute | solution.py:110
  86.3 1.0 constant_dynamic-update-slice_fusion.6
  87.2 1.0 constant_dynamic-update-slice_fusion.5
  88.2 1.0 constant_dynamic-update-slice_fusion.3
  89.2 1.0 constant_dynamic-update-slice_fusion.2
  90.7 1.2 copy-done.1
  93.2 3.3 %fusion = bf16[128,3072]{1,0:T(8,128)(2,1)} fusion(bf16[4,128,3072]{2,1,0:T(8,128)(2,1)S(1)} %copy-done, f32[128,4,128]{0,2,1:T(8,128)S(1)} %fusion.7, f32[128,4,512]{0,2,1:T(8,128)} %copy-done.1, bf16[1024,4,256]{2,0,1:T(8,128)(2,1)} %copy-done.7, s32[]{:T(128)S(6)} %select_n.75, s32[]{:T(128)S(6)} %add.115, f32[128,4]{0,1:T(4,128)S(1)} %get-tuple-element.10, ...), kind=kOutput, calls=%fused_computation.1 | convolution fusion | flops 471138304 | bytes 5771784 | tf_op jit(solution)/shard_map/dot_general | solution.py:125
  96.5 1.0 slice.61
  97.7 8.4 %all_to_all.36 = bf16[128,4,256]{2,1,0:T(4,128)(2,1)S(1)} all-to-all(bf16[128,4,256]{2,1,0:T(4,128)(2,1)S(1)} %copy.26), channel_id=1, replica_groups=mesh['clip'=2,'patch'=4,'head'=2,'rep'=2] {'head','rep'}, dimensions={0} | all-to-all | bytes 524288 | tf_op jit(solution)/shard_map/all_to_all | solution.py:93
  107.0 10.5 %reduce-scatter.2.cloned.1.call-done = bf16[32,3072]{1,0:T(8,128)(2,1)} async-done(((bf16[128,3072]{1,0:T(8,128)(2,1)}), bf16[32,3072]{1,0:T(8,128)(2,1)}) %reduce-scatter.2.cloned.1.call-update) | async-done | bytes 196624 | tf_op jit(solution)/shard_map/reduce_scatter | solution.py:124
  117.5 1.6 %multiply_convert_fusion = bf16[32,3072]{1,0:T(8,128)(2,1)} fusion(bf16[32,3072]{1,0:T(8,128)(2,1)} %reduce-scatter.2.cloned.1.call-done, f32[3072]{0:T(1024)S(1)} %bitcast.52), kind=kLoop, calls=%fused_computation.33 | loop fusion | flops 294912 | bytes 405504 | tf_op jit(solution)/shard_map/convert_element_type | solution.py:130
  (57 shorter events, 8.0 us)
Async XLA Ops:
  7.2 86.0 %copy-start = (bf16[4,128,3072]{2,1,0:T(8,128)(2,1)S(1)}, bf16[4,128,3072]{2,1,0:T(8,128)(2,1)}, u32[]{:S(2)}) copy-start(bf16[4,128,3072]{2,1,0:T(8,128)(2,1)} %param.13) | copy-start | bytes 9437188
  9.1 45.2 %all-to-all-start = ((bf16[32,16,256]{2,0,1:T(8,128)(2,1)}), bf16[32,16,256]{2,0,1:T(8,128)(2,1)}, u32[]{:S(2)}, u32[]{:S(2)}) async-start(bf16[32,16,256]{2,0,1:T(8,128)(2,1)} %copy.21), calls=%async_computation | async-start | bytes 524288 | tf_op jit(solution)/shard_map/all_to_all | solution.py:105
  13.3 104.2 %reduce-scatter.2.cloned.1.call-start = ((), (), s32[]{:S(2)}) async-start(), calls=%async_computation.3 | async-start | bytes 983040 | tf_op jit(solution)/shard_map/reduce_scatter | solution.py:124
  22.3 12.8 %copy-start.8 = (f32[3,3072]{1,0:T(4,128)S(1)}, f32[3,3072]{1,0:T(4,128)}, u32[]{:S(2)}) copy-start(f32[3,3072]{1,0:T(4,128)} %param.9) | copy-start | bytes 110596
  22.3 12.8 %copy-start.4 = (bf16[32,3072]{1,0:T(8,128)(2,1)S(1)}, bf16[32,3072]{1,0:T(8,128)(2,1)}, u32[]{:S(2)}) copy-start(bf16[32,3072]{1,0:T(8,128)(2,1)} %param.8) | copy-start | bytes 589828
  45.5 8.0 %copy-start.12 = (s32[4]{0:T(128)S(1)}, s32[4]{0:T(128)}, u32[]{:S(2)}) copy-start(s32[4]{0:T(128)} %param.15) | copy-start | bytes 52
  52.5 0.9 copy-start.2
  55.2 10.9 %collective-permute-start = (bf16[128,4,256]{2,0,1:T(8,128)(2,1)S(1)}, bf16[128,4,256]{2,0,1:T(8,128)(2,1)S(1)}, u32[]{:S(2)}, u32[]{:S(2)}) collective-permute-start(bf16[128,4,256]{2,0,1:T(8,128)(2,1)S(1)} %bitcast.48), channel_id=1, source_target_pairs={{0,4},{4,8},{8,12},{12,0},{1,5},{5,9},{9,13},{13,1},{2,6},{6,10},{... | collective-permute-start | bytes 786440 | tf_op jit(solution)/shard_map/ppermute | solution.py:110
  66.1 0.7 copy-start.5
  66.2 9.9 %collective-permute-start.1 = (bf16[128,4,256]{2,0,1:T(8,128)(2,1)S(1)}, bf16[128,4,256]{2,0,1:T(8,128)(2,1)}, u32[]{:S(2)}, u32[]{:S(2)}) collective-permute-start(bf16[128,4,256]{2,0,1:T(8,128)(2,1)S(1)} %collective-permute-done), channel_id=1, source_target_pairs={{0,4},{4,8},{8,12},{12,0},{1,5},{5,9},{9,13},{13,1},{2,6},{6,10},{... | collective-permute-start | bytes 786440 | tf_op jit(solution)/shard_map/ppermute | solution.py:110
  76.0 9.2 %collective-permute-start.2 = (bf16[128,4,256]{2,0,1:T(8,128)(2,1)}, bf16[128,4,256]{2,0,1:T(8,128)(2,1)}, u32[]{:S(2)}, u32[]{:S(2)}) collective-permute-start(bf16[128,4,256]{2,0,1:T(8,128)(2,1)} %collective-permute-done.1), channel_id=1, source_target_pairs={{0,4},{4,8},{8,12},{12,0},{1,5},{5,9},{9,13},{13,1},{2,6},{6,10},{... | collective-permute-start | bytes 786440 | tf_op jit(solution)/shard_map/ppermute | solution.py:110
  77.2 13.0 %copy-start.6 = (bf16[128,4,256]{2,0,1:T(8,128)(2,1)S(1)}, bf16[128,4,256]{2,0,1:T(8,128)(2,1)}, u32[]{:S(2)}) copy-start(bf16[128,4,256]{2,0,1:T(8,128)(2,1)} %copy-done.5) | copy-start | bytes 786436
  78.5 11.8 %copy-start.3 = (f32[128,4,384]{2,0,1:T(8,128)S(1)}, f32[128,4,384]{2,0,1:T(8,128)}, u32[]{:S(2)}) copy-start(f32[128,4,384]{2,0,1:T(8,128)} %copy-done.2) | copy-start | bytes 2359300
  78.5 11.8 %copy-start.9 = (pred[512]{0:T(512)(128)(4,1)S(1)}, pred[512]{0:T(512)(128)(4,1)}, u32[]{:S(2)}) copy-start(pred[512]{0:T(512)(128)(4,1)} %compare_and_fusion) | copy-start | bytes 1540
  78.5 11.8 %copy-start.11 = (f32[128]{0:T(128)S(1)}, f32[128]{0:T(128)}, u32[]{:S(2)}) copy-start(f32[128]{0:T(128)} %param.11) | copy-start | bytes 1540
  90.2 2.0 %copy-start.10 = (pred[128]{0:T(512)(128)(4,1)S(1)}, pred[128]{0:T(512)(128)(4,1)}, u32[]{:S(2)}) copy-start(pred[128]{0:T(512)(128)(4,1)} %iota_compare_fusion.1) | copy-start | bytes 388
  90.3 2.9 %copy-start.7 = (bf16[1024,4,256]{2,0,1:T(8,128)(2,1)}, bf16[1024,4,256]{2,0,1:T(8,128)(2,1)S(1)}, u32[]{:S(2)}) copy-start(bf16[1024,4,256]{2,0,1:T(8,128)(2,1)S(1)} %constant_dynamic-update-slice_fusion) | copy-start | bytes 6291460
  90.7 1.2 copy-start.1
Sparse Core Ops, SparseCore 0:
  96.6 20.8 reduce-scatter.1
